TPU v7x, 32 devices: a whole 2x2x4 slice. The times are simulated.
32 devices in a mesh: group: 2 (over x), seq: 16 (over z, y, core).
Axes of the slice: x: 2, y: 2, z: 4, core: 2. Of those that a mesh axis runs over, the one named last changes fastest.
Arguments:
- queries: bfloat16 [8192, 768], P(('group', 'seq')), parts along dimension 0, may hold values from -6 to 6
- key_rows: bfloat16 [8192, 768], P(('group', 'seq')), parts along dimension 0, may hold values from -6 to 6
- value_rows: bfloat16 [8192, 768], P(('group', 'seq')), parts along dimension 0, may hold values from -20 to 20
- dilation: int32 [12], replicated, may hold values from 2 to 30, as said below
- global_rows: int32 [128], P('group'), parts along dimension 0, may hold values from 0 to 4095, as said below
- out_weight: bfloat16 [768, 1536], replicated, may hold values from -0.21875 to 0.21875
- mlp_up: bfloat16 [1536, 3072], P('seq'), may hold values from -0.15625 to 0.15625
- mlp_down: bfloat16 [3072, 1536], P('seq'), may hold values from -0.109375 to 0.109375
Outputs:
- attended: bfloat16 [8192, 1536], P(('group', 'seq')), parts along dimension 0
- mlp_out: bfloat16 [8192, 1536], P(('group', 'seq')), parts along dimension 0
There are 2 independent parts, one for each index of `group`. A program takes and returns all parts, laid end to end along the dimension named above; an argument that names none is the same for every part. Nothing has to cross between parts.
Inputs may be any that keep to these rules, and one draw needn't show every extreme that they name: `dilation`: each offset is a multiple of 2; some head has the smallest and some the largest. `global_rows`: distinct positions.
All inputs are finite; a program needn't handle non-finite values.
Results may differ from a plain program's by a relative error of at most 0.0071.
Values may be sent and summed in bfloat16 or wider, within the bound.
A program may use at most 192 MiB of HBM per device.

v0:
```python
import jax
import jax.numpy as jnp
from jax import lax
from jax.sharding import PartitionSpec as P

H = 12
DH = 64
BLK = 128
GLOBALS = 64


def with_halo(cells, sides, width):
    for axis, dim in sides:
        count = lax.axis_size(axis)
        head = lax.slice_in_dim(cells, 0, width, axis=dim)
        tail = lax.slice_in_dim(cells, cells.shape[dim] - width, cells.shape[dim], axis=dim)
        cells = jnp.concatenate(
            [
                lax.ppermute(tail, axis, [(i, (i + 1) % count) for i in range(count)]),
                cells,
                lax.ppermute(head, axis, [((i + 1) % count, i) for i in range(count)]),
            ],
            axis=dim,
        )
    return cells


def passed_along(value, axis, steps):
    count = lax.axis_size(axis)
    pairs = [(source, (source + steps) % count) for source in range(count)]
    return lax.ppermute(value, axis, pairs)


def merged_2(part, axis, combine):
    gathered = jax.tree.map(lambda a: lax.all_gather(a, axis), part)

    def take(source):
        return jax.tree.map(lambda a: lax.dynamic_index_in_dim(a, source, 0, False), gathered)

    return lax.fori_loop(
        1, lax.axis_size(axis), lambda source, state: combine(state, take(source)), take(0)
    )


def attend_blocks(query_blocks, local_keys, local_values, glob_keys, glob_values):
    count = query_blocks.shape[0]
    keys_all = jnp.concatenate(
        [local_keys, jnp.broadcast_to(glob_keys[None], (count,) + glob_keys.shape)], axis=1
    )
    values_all = jnp.concatenate(
        [local_values, jnp.broadcast_to(glob_values[None], (count,) + glob_values.shape)], axis=1
    )
    scores = jnp.einsum(
        "nqhd,nkhd->nhqk", query_blocks, keys_all, preferred_element_type=jnp.float32
    ) * DH ** (-0.5)
    peak = jnp.max(scores, axis=-1, keepdims=True)
    exp_terms = jnp.exp(scores - peak)
    totals = jnp.sum(exp_terms, axis=-1, keepdims=True)
    weights = (exp_terms / totals).astype(jnp.bfloat16)
    return jnp.einsum("nhqk,nkhd->nqhd", weights, values_all, preferred_element_type=jnp.float32)


def select_heads(chosen, arrived, current):
    shaped = current.shape
    head_mask = chosen[None, None, :, None]
    merged = jnp.where(
        head_mask,
        arrived.reshape(shaped[0], shaped[1], H, DH),
        current.reshape(shaped[0], shaped[1], H, DH),
    )
    return merged.reshape(shaped)


def join_partials(first, second):
    peak_first, total_first, numer_first = first
    peak_second, total_second, numer_second = second
    highest = jnp.maximum(peak_first, peak_second)
    scale_first = jnp.exp(peak_first - highest)
    scale_second = jnp.exp(peak_second - highest)
    return (
        highest,
        total_first * scale_first + total_second * scale_second,
        numer_first * scale_first[:, :, None] + numer_second * scale_second[:, :, None],
    )


def per_device(queries, key_rows, value_rows, dilation, global_rows, out_weight, mlp_up, mlp_down):
    tok_rows = queries.shape[0]
    blocks = tok_rows // BLK
    devices = lax.axis_size("seq")
    stacked = jnp.stack([key_rows, value_rows])
    padded = with_halo(stacked, (("seq", 1),), BLK)
    dev_hops = dilation // blocks
    current = stacked
    for bit_level in range((devices - 1).bit_length()):
        arrived = passed_along(current, "seq", -(1 << bit_level))
        chosen = dev_hops >> bit_level & 1 == 1
        current = select_heads(chosen, arrived, current)
    start = lax.axis_index("seq") * tok_rows
    offsets = global_rows - start
    onehot = offsets[:, None] == jnp.arange(tok_rows, dtype=jnp.int32)[None, :]
    picker = onehot.astype(jnp.bfloat16)
    picked = (
        jnp.dot(picker, queries, preferred_element_type=jnp.float32),
        jnp.dot(picker, key_rows, preferred_element_type=jnp.float32),
        jnp.dot(picker, value_rows, preferred_element_type=jnp.float32),
    )
    glob_q, glob_k, glob_v = lax.psum((picked[0], picked[1], picked[2]), "seq")
    glob_query = glob_q.astype(jnp.bfloat16).reshape(GLOBALS, H, DH)
    glob_keys = glob_k.astype(jnp.bfloat16).reshape(GLOBALS, H, DH)
    glob_values = glob_v.astype(jnp.bfloat16).reshape(GLOBALS, H, DH)
    grid = padded.reshape(2, blocks + 2, BLK, H, DH)
    dilated = current.reshape(2, blocks, BLK, H, DH)
    local_set = jnp.concatenate([grid[:, :-2], grid[:, 1:-1], grid[:, 2:], dilated], axis=2)
    attended_local = attend_blocks(
        queries.reshape(blocks, BLK, H, DH), local_set[0], local_set[1], glob_keys, glob_values
    ).reshape(tok_rows, H * DH)
    scores = jnp.einsum(
        "ghd,thd->hgt",
        glob_query,
        key_rows.reshape(tok_rows, H, DH),
        preferred_element_type=jnp.float32,
    ) * DH ** (-0.5)
    peak = jnp.max(scores, axis=2)
    exp_terms = jnp.exp(scores - peak[:, :, None])
    totals = jnp.sum(exp_terms, axis=2)
    numerators = jnp.einsum(
        "hgt,thd->hgd",
        exp_terms,
        value_rows.astype(jnp.float32).reshape(tok_rows, H, DH),
        precision=lax.Precision.HIGHEST,
    )
    peak, totals, numerators = merged_2((peak, totals, numerators), "seq", join_partials)
    glob_out = (numerators / totals[:, :, None]).transpose(1, 0, 2).reshape(GLOBALS, H * DH)
    onehot_float = onehot.astype(jnp.float32)
    placed = jnp.dot(onehot_float.T, glob_out, precision=lax.Precision.HIGHEST)
    owned_rows = jnp.sum(onehot_float, axis=0) > 0.5
    attention = jnp.where(owned_rows[:, None], placed, attended_local).astype(jnp.bfloat16)
    attended = jnp.dot(attention, out_weight, preferred_element_type=jnp.float32).astype(
        jnp.bfloat16
    )
    columns = attended
    pre_act = jnp.dot(
        columns,
        lax.all_gather(mlp_up, "seq", axis=0, tiled=True),
        preferred_element_type=jnp.float32,
    )
    hidden = jax.nn.gelu(pre_act, approximate=True).astype(jnp.bfloat16)
    columns = hidden
    mlp_out = jnp.dot(
        columns,
        lax.all_gather(mlp_down, "seq", axis=0, tiled=True),
        preferred_element_type=jnp.float32,
    ).astype(jnp.bfloat16)
    return (attended, mlp_out)


def solution(mesh):
    placed = (
        P(("group", "seq"), None),
        P(("group", "seq"), None),
        P(("group", "seq"), None),
        P(),
        P("group"),
        P(),
        P("seq", None),
        P("seq", None),
    )
    return jax.shard_map(
        per_device,
        mesh=mesh,
        in_specs=placed,
        out_specs=(P(("group", "seq"), None), P(("group", "seq"), None)),
        check_vma=False,
    )
```

profile of v0, /device:TPU:1, one launch (start us, length us, event | category | flops | bytes accessed | tf_op | source)
XLA Modules:
  0.0 397.4 jit_solution(10071234965016458596)
XLA Ops:
  15.0 2.0 fusion.49
  17.0 64.9 %all-reduce.2 = (bf16[64,768]{1,0:T(8,128)(2,1)}, bf16[64,768]{1,0:T(8,128)(2,1)}, bf16[64,768]{1,0:T(8,128)(2,1)}) all-reduce(f32[64,768]{1,0:T(8,128)} %fusion.47, f32[64,768]{1,0:T(8,128)} %fusion.48, f32[64,768]{1,0:T(8,128)} %fusion.49), channel_id=1, replica_groups=mesh['group'=2,'seq'=16] {'seq'}, use_global_device_ids=true, to_apply=%region_7.8 | all-reduce | flops 147456 | bytes 884736 | tf_op jit(solution)/shard_map/psum | solution.py:108
  85.9 2.4 fusion.37
  90.7 5.3 %collective-permute-start.2 = (bf16[2,256,768]{2,1,0:T(8,128)(2,1)}, bf16[2,256,768]{2,1,0:T(8,128)(2,1)}, u32[]{:S(2)}, u32[]{:S(2)}) collective-permute-start(bf16[2,256,768]{2,1,0:T(8,128)(2,1)} %pad_maximum_fusion.9), channel_id=1, source_target_pairs={{0,15},{1,0},{2,1},{3,2},{4,3},{5,4},{6,5},{7,6},{8,7},{9,8},{10,9... | collective-permute-start | bytes 2359304 | tf_op jit(solution)/shard_map/ppermute | solution.py:31
  97.9 7.5 %collective-permute-done.2 = bf16[2,256,768]{2,1,0:T(8,128)(2,1)} collective-permute-done((bf16[2,256,768]{2,1,0:T(8,128)(2,1)}, bf16[2,256,768]{2,1,0:T(8,128)(2,1)}, u32[]{:S(2)}, u32[]{:S(2)}) %collective-permute-start.2) | collective-permute-done | bytes 786464 | tf_op jit(solution)/shard_map/ppermute | solution.py:31
  105.4 2.1 broadcast_select_fusion
  107.5 16.6 %collective-permute-start.3 = (bf16[2,256,768]{2,1,0:T(8,128)(2,1)}, bf16[2,256,768]{2,1,0:T(8,128)(2,1)}, u32[]{:S(2)}, u32[]{:S(2)}) collective-permute-start(bf16[2,256,768]{2,1,0:T(8,128)(2,1)} %broadcast_select_fusion), channel_id=1, source_target_pairs={{0,14},{1,15},{2,0},{3,1},{4,2},{5,3},{6,4},{7,5},{8,6},{9,7},{10,... | collective-permute-start | bytes 2359304 | tf_op jit(solution)/shard_map/ppermute | solution.py:31
  125.4 28.2 %collective-permute-done.3 = bf16[2,256,768]{2,1,0:T(8,128)(2,1)} collective-permute-done((bf16[2,256,768]{2,1,0:T(8,128)(2,1)}, bf16[2,256,768]{2,1,0:T(8,128)(2,1)}, u32[]{:S(2)}, u32[]{:S(2)}) %collective-permute-start.3) | collective-permute-done | bytes 786464 | tf_op jit(solution)/shard_map/ppermute | solution.py:31
  153.6 2.4 broadcast_select_fusion.1
  160.2 2.0 copy.89
  172.5 27.9 %all-gather.4 = f32[16,12,64]{2,1,0:T(8,128)S(1)} all-gather(f32[1,12,64]{2,1,0:T(8,128)S(1)} %bitcast.103), channel_id=3, replica_groups=mesh['group'=2,'seq'=16] {'seq'}, dimensions={0}, use_global_device_ids=true | all-gather | bytes 52224 | tf_op jit(solution)/shard_map/all_gather | solution.py:35
  200.4 18.3 %all-gather.3 = f32[16,12,64]{2,1,0:T(8,128)S(1)} all-gather(f32[1,12,64]{2,1,0:T(8,128)S(1)} %bitcast.102), channel_id=2, replica_groups=mesh['group'=2,'seq'=16] {'seq'}, dimensions={0}, use_global_device_ids=true | all-gather | bytes 52224 | tf_op jit(solution)/shard_map/all_gather | solution.py:35
  219.4 2.4 broadcast_select_fusion.2
  222.4 2.4 pad_maximum_fusion.2
  224.8 2.6 copy.71
  227.4 3.5 reshape.91
  230.9 5.1 %fusion.65 = (bf16[2,2,128,12,64]{2,1,4,3,0:T(2,128)(2,1)S(1)}, bf16[2,2,128,12,64]{2,1,4,3,0:T(2,128)(2,1)S(1)}, bf16[2,2,128,12,64]{2,1,4,3,0:T(2,128)(2,1)S(1)}) fusion(bf16[2,4,128,12,64]{2,1,4,3,0:T(4,128)(2,1)} %reshape.91), kind=kLoop, calls=%fused_computation.98 | loop fusion | bytes 4718592 | tf_op jit(solution)/shard_map/slice | solution.py:114
  238.5 2.3 copy.78
  240.8 2.7 reshape.95
  243.5 2.3 copy.77
  245.8 2.7 reshape.94
  248.5 2.3 copy.76
  250.8 2.7 reshape.93
  253.5 39.1 %collective-permute-done.5 = bf16[2,256,768]{2,1,0:T(8,128)(2,1)} collective-permute-done((bf16[2,256,768]{2,1,0:T(8,128)(2,1)}, bf16[2,256,768]{2,1,0:T(8,128)(2,1)}, u32[]{:S(2)}, u32[]{:S(2)}) %collective-permute-start.5) | collective-permute-done | bytes 786464 | tf_op jit(solution)/shard_map/ppermute | solution.py:31
  292.7 2.3 copy.75
  294.9 2.7 reshape.92
  297.7 2.6 fusion.36
  303.0 7.2 %fusion.66 = (f32[2,12,128]{2,1,0:T(8,128)S(1)}, f32[2,12,128,576]{2,3,1,0:T(8,128)}) fusion(bf16[2,64,12,64]{1,3,2,0:T(8,128)(2,1)S(1)} %broadcast_in_dim.97, bf16[2,512,12,64]{1,3,2,0:T(8,128)(2,1)} %get-tuple-element.205, bf16[2,128,12,64]{1,0,3,2:T(2,128)(2,1)S(1)} %copy-done.8), kind=kOutput, calls=%fused_computation.99 | convolution fusion | flops 235340352 | bytes 9252864 | tf_op jit(solution)/shard_map/sub | solution.py:57
  310.3 4.3 %fusion.30 = bf16[2,128,12,64]{1,3,2,0:T(8,128)(2,1)S(1)} fusion(f32[2,12,128,576]{2,3,1,0:T(8,128)} %get-tuple-element.215, f32[2,12,128]{2,1,0:T(8,128)S(1)} %get-tuple-element.214, bf16[2,64,12,64]{1,3,2,0:T(8,128)(2,1)S(1)} %broadcast_in_dim.95, bf16[2,512,12,64]{1,3,2,0:T(8,128)(2,1)} %get-tuple-element.204), kind=kOutput, calls=%fused_computation.42 | convolution fusion | flops 233570304 | bytes 9252864 | tf_op jit(solution)/shard_map/nhqk,nkhd->nqhd/dot_general | solution.py:60
  316.3 32.2 %while.19 = (s32[]{:T(128)}, f32[12,64]{1,0:T(8,128)S(1)}, f32[12,64]{1,0:T(8,128)S(1)}, f32[12,64,64]{2,1,0:T(8,128)S(1)}, f32[16,12,64]{2,1,0:T(8,128)}, /*ind...) while((s32[]{:T(128)}, f32[12,64]{1,0:T(8,128)S(1)}, ...), condition=%wide.region_5.6_spmd, body=%wide.region_4.5_spmd.sunk | while | flops 152069 | bytes 620695 | solution.py:40
  350.5 27.9 %all-gather.9.cloned.1.call-done = bf16[1536,3072]{1,0:T(8,128)(2,1)} async-done(((bf16[96,3072]{1,0:T(8,128)(2,1)}), bf16[1536,3072]{1,0:T(8,128)(2,1)}) %all-gather.9.cloned.1.call-update) | async-done | bytes 9437200 | tf_op jit(solution)/shard_map/all_gather | solution.py:145
  378.4 12.4 %convolution_convert_fusion = bf16[256,1536]{1,0:T(8,128)(2,1)} fusion(bf16[3072,1536]{1,0:T(8,128)(2,1)} %all-gather.11.cloned.1.call-done, bf16[256,1536]{1,0:T(8,128)(2,1)S(1)} %convolution_convert_fusion.1, bf16[1536,3072]{1,0:T(8,128)(2,1)} %all-gather.9.cloned.1.call-done), kind=kOutput, calls=%fused_computation.28 | convolution fusion | flops 4839309312 | bytes 20447232 | tf_op jit(solution)/shard_map/dot_general | solution.py:150
  (128 shorter events, 73.9 us)
Async XLA Ops:
  7.2 342.5 %copy-start = (bf16[768,1536]{1,0:T(8,128)(2,1)S(1)}, bf16[768,1536]{1,0:T(8,128)(2,1)}, u32[]{:S(2)}) copy-start(bf16[768,1536]{1,0:T(8,128)(2,1)} %param.15) | copy-start | bytes 7077892
  7.2 308.1 %all-gather.13.cloned.1.call-start = ((), (), s32[]{:S(2)}) async-start(), calls=%async_computation.2 | async-start | bytes 6684672 | tf_op jit(solution)/shard_map/all_gather | solution.py:35
  9.2 74.5 %copy-start.11 = (s32[64]{0:T(128)}, s32[64]{0:T(128)S(1)}, u32[]{:S(2)}) copy-start(s32[64]{0:T(128)S(1)} %broadcast_subtract_fusion) | copy-start | bytes 772
  15.0 74.8 %copy-start.1 = (bf16[256,768]{1,0:T(8,128)(2,1)S(1)}, bf16[256,768]{1,0:T(8,128)(2,1)}, u32[]{:S(2)}) copy-start(bf16[256,768]{1,0:T(8,128)(2,1)} %param.11) | copy-start | bytes 1179652
  15.0 74.8 %copy-start.2 = (bf16[256,768]{1,0:T(8,128)(2,1)S(1)}, bf16[256,768]{1,0:T(8,128)(2,1)}, u32[]{:S(2)}) copy-start(bf16[256,768]{1,0:T(8,128)(2,1)} %param.12) | copy-start | bytes 1179652
  83.7 12.3 %copy-start.17 = (s32[12]{0:T(128)S(1)}, s32[12]{0:T(128)}, u32[]{:S(2)}) copy-start(s32[12]{0:T(128)} %param.13) | copy-start | bytes 148
  85.0 0.9 copy-start.3
  88.3 262.2 %all-gather.11.cloned.1.call-start = ((), (), s32[]{:S(2)}) async-start(), calls=%async_computation.1 | async-start | bytes 10027008 | tf_op jit(solution)/shard_map/all_gather | solution.py:152
  89.0 289.4 %all-gather.9.cloned.1.call-start = ((), (), s32[]{:S(2)}) async-start(), calls=%async_computation | async-start | bytes 10027008 | tf_op jit(solution)/shard_map/all_gather | solution.py:145
  90.7 14.6 %collective-permute-start.2 = (bf16[2,256,768]{2,1,0:T(8,128)(2,1)}, bf16[2,256,768]{2,1,0:T(8,128)(2,1)}, u32[]{:S(2)}, u32[]{:S(2)}) collective-permute-start(bf16[2,256,768]{2,1,0:T(8,128)(2,1)} %pad_maximum_fusion.9), channel_id=1, source_target_pairs={{0,15},{1,0},{2,1},{3,2},{4,3},{5,4},{6,5},{7,6},{8,7},{9,8},{10,9... | collective-permute-start | bytes 2359304 | tf_op jit(solution)/shard_map/ppermute | solution.py:31
  97.1 0.6 copy-start.15
  107.5 46.1 %collective-permute-start.3 = (bf16[2,256,768]{2,1,0:T(8,128)(2,1)}, bf16[2,256,768]{2,1,0:T(8,128)(2,1)}, u32[]{:S(2)}, u32[]{:S(2)}) collective-permute-start(bf16[2,256,768]{2,1,0:T(8,128)(2,1)} %broadcast_select_fusion), channel_id=1, source_target_pairs={{0,14},{1,15},{2,0},{3,1},{4,2},{5,3},{6,4},{7,5},{8,6},{9,7},{10,... | collective-permute-start | bytes 2359304 | tf_op jit(solution)/shard_map/ppermute | solution.py:31
  125.4 36.8 %copy-start.14 = (pred[12]{0:T(512)(128)(4,1)S(1)}, pred[12]{0:T(512)(128)(4,1)}, u32[]{:S(2)}) copy-start(pred[12]{0:T(512)(128)(4,1)} %get-tuple-element.211) | copy-start | bytes 40
  155.9 63.5 %collective-permute-start.4 = (bf16[2,256,768]{2,1,0:T(8,128)(2,1)}, bf16[2,256,768]{2,1,0:T(8,128)(2,1)}, u32[]{:S(2)}, u32[]{:S(2)}) collective-permute-start(bf16[2,256,768]{2,1,0:T(8,128)(2,1)} %broadcast_select_fusion.1), channel_id=1, source_target_pairs={{0,12},{1,13},{2,14},{3,15},{4,0},{5,1},{6,2},{7,3},{8,4},{9,5},{1... | collective-permute-start | bytes 2359304 | tf_op jit(solution)/shard_map/ppermute | solution.py:31
  156.9 65.5 %collective-permute-start = (bf16[2,128,768]{2,1,0:T(8,128)(2,1)}, bf16[2,128,768]{2,1,0:T(8,128)(2,1)}, u32[]{:S(2)}, u32[]{:S(2)}) collective-permute-start(bf16[2,128,768]{2,1,0:T(8,128)(2,1)} %get-tuple-element.209), channel_id=1, source_target_pairs={{0,1},{1,2},{2,3},{3,4},{4,5},{5,6},{6,7},{7,8},{8,9},{9,10},{10,1... | collective-permute-start | bytes 1179656 | tf_op jit(solution)/shard_map/ppermute | solution.py:19
  156.9 61.8 %copy-start.12 = (s32[64]{0:T(128)S(1)}, s32[64]{0:T(128)}, u32[]{:S(2)}) copy-start(s32[64]{0:T(128)} %copy-done.11) | copy-start | bytes 772
  156.9 65.5 %collective-permute-start.1 = (bf16[2,128,768]{2,1,0:T(8,128)(2,1)}, bf16[2,128,768]{2,1,0:T(8,128)(2,1)}, u32[]{:S(2)}, u32[]{:S(2)}) collective-permute-start(bf16[2,128,768]{2,1,0:T(8,128)(2,1)} %get-tuple-element.210), channel_id=1, source_target_pairs={{1,0},{2,1},{3,2},{4,3},{5,4},{6,5},{7,6},{8,7},{9,8},{10,9},{11,1... | collective-permute-start | bytes 1179656 | tf_op jit(solution)/shard_map/ppermute | solution.py:21
  200.4 18.4 %copy-start.9 = (f32[16,12,64]{2,1,0:T(8,128)}, f32[16,12,64]{2,1,0:T(8,128)S(1)}, u32[]{:S(2)}) copy-start(f32[16,12,64]{2,1,0:T(8,128)S(1)} %all-gather.4) | copy-start | bytes 147460
  218.7 0.7 copy-start.10
  221.8 70.8 %collective-permute-start.5 = (bf16[2,256,768]{2,1,0:T(8,128)(2,1)}, bf16[2,256,768]{2,1,0:T(8,128)(2,1)}, u32[]{:S(2)}, u32[]{:S(2)}) collective-permute-start(bf16[2,256,768]{2,1,0:T(8,128)(2,1)} %broadcast_select_fusion.2), channel_id=1, source_target_pairs={{0,8},{1,9},{2,10},{3,11},{4,12},{5,13},{6,14},{7,15},{8,0},{9,1},... | collective-permute-start | bytes 2359304 | tf_op jit(solution)/shard_map/ppermute | solution.py:31
  297.6 2.6 copy-start.4
  297.6 2.6 copy-start.5
  301.0 1.9 copy-start.7
  301.0 2.0 copy-start.8
  302.9 7.2 %copy-start.6 = (bf16[64,768]{0,1:T(8,128)(2,1)S(1)}, bf16[64,768]{0,1:T(8,128)(2,1)}, u32[]{:S(2)}) copy-start(bf16[64,768]{0,1:T(8,128)(2,1)} %copy.93) | copy-start | bytes 294916
  316.3 32.8 %copy-start.13 = (s32[64]{0:T(128)S(1)}, s32[64]{0:T(128)}, u32[]{:S(2)}) copy-start(s32[64]{0:T(128)} %copy-done.11) | copy-start | bytes 772
  316.3 32.8 %copy-start.16 = (pred[256]{0:T(512)(128)(4,1)S(1)}, pred[256]{0:T(512)(128)(4,1)}, u32[]{:S(2)}) copy-start(pred[256]{0:T(512)(128)(4,1)} %broadcast_compare_fusion) | copy-start | bytes 772
  350.5 40.4 %copy-start.18 = (bf16[256,1536]{1,0:T(8,128)(2,1)}, bf16[256,1536]{1,0:T(8,128)(2,1)S(1)}, u32[]{:S(2)}) copy-start(bf16[256,1536]{1,0:T(8,128)(2,1)S(1)} %convolution_convert_fusion.1) | copy-start | bytes 2359300
Sparse Core Ops, SparseCore 0:
  88.4 88.6 all-gather.12
  179.3 116.2 all-gather.10
  297.9 80.4 all-gather.8
where the time goes:
time: 400 us; the launch traced here: 397 us
  blocking collectives  111 us (28%)
  waiting for transfers between devices  104 us (26%)
  local copies, waits for them, and re-layouts  60.1 us (15%)
  other arithmetic  50.4 us (13%)
  matrix products  34.8 us (9%)
  starting transfers between devices  22.5 us (6%)
  between operations  14.1 us (4%)
    ppermute x4, waiting for transfers between devices, passed_along(): return lax.ppermute(value, axis, pairs)  74.8 us
    psum x1, blocking collectives, per_device(): glob_q, glob_k, glob_v = lax.psum((picked[0], picked[1], picked[2]), 'seq')  64.9 us
    all_gather x2, blocking collectives, merged_2(): gathered = jax.tree.map(lambda a: lax.all_gather(a, axis), part)  46.2 us
    all_gather x1, waiting for transfers between devices, per_device(): lax.all_gather(mlp_up, 'seq', axis=0, tiled=True)  27.9 us
    ppermute x4, starting transfers between devices, passed_along(): return lax.ppermute(value, axis, pairs)  21.8 us
    add x15, other arithmetic, join_partials(): numer_first * scale_first[:, :, None]  20.8 us
    dot_general x1, matrix products, per_device(): jnp.dot(columns, lax.all_gather(mlp_down, 'seq', axis=0, tiled=True), pre...  12.4 us
    add x15, other arithmetic, join_partials(): total_first * scale_first + total_second * scale_second  11 us
  transfers between devices with their start and end apart: 9, of which 4 were waited for; matrix products, arithmetic and copies ran while one was open for 29% of the time, Pallas kernels for 0%

commit v1 on v0

v1 whole, which is shorter than its diff:
```python
import functools

import jax
import jax.numpy as jnp
from jax import lax
from jax.experimental import pallas as pl
from jax.experimental.pallas import tpu as pltpu
from jax.sharding import PartitionSpec as P

H = 12
DH = 64
BLK = 128
GLOBALS = 64
LANES = 2 * DH
PAIRS = H // 2
CHUNK = 1024


def split_pair(rows):
    lane = lax.broadcasted_iota(jnp.int32, rows.shape, 1)
    zero = jnp.zeros_like(rows)
    return jnp.concatenate(
        [jnp.where(lane < DH, rows, zero), jnp.where(lane < DH, zero, rows)], axis=0
    )


def join_pair(first, second):
    lane = lax.broadcasted_iota(jnp.int32, first.shape, 1)
    return jnp.where(lane < DH, first, second)


def dot_t(left, right):
    return lax.dot_general(
        left, right, (((1,), (1,)), ((), ())), preferred_element_type=jnp.float32
    )


def dot(left, right):
    return jnp.dot(left, right, preferred_element_type=jnp.float32)


def attention_kernel(
    length, scal, q_ref, col_ref, row_ref, kc_ref, vc_ref, k_hbm, v_hbm, out_ref,
    loc_k, loc_v, dil_k, dil_v, gq, gk, gv, top, total, acc, sems,
):
    step = pl.program_id(0)
    tok = q_ref.shape[0]
    chunk = kc_ref.shape[0]
    me = scal[H]
    start = me * tok

    def copies():
        made = []
        spans = [
            (lax.rem(start + length - BLK, length), 0, BLK),
            (start, BLK, tok),
            (lax.rem(start + tok, length), BLK + tok, BLK),
        ]
        for hbm, loc, dil in ((k_hbm, loc_k, dil_k), (v_hbm, loc_v, dil_v)):
            for source, target, size in spans:
                rows = pl.ds(pl.multiple_of(source, BLK), size)
                made.append((hbm.at[rows, :], loc.at[pl.ds(target, size), :]))
            for head in range(H):
                source = lax.rem(start + scal[head] * BLK, length)
                rows = pl.ds(pl.multiple_of(source, BLK), tok)
                made.append((hbm.at[rows, pl.ds(head // 2 * LANES, LANES)], dil.at[head]))
        return [
            pltpu.make_async_copy(source, target, sems.at[at])
            for at, (source, target) in enumerate(made)
        ]

    @pl.when(step == 0)
    def _():
        for copy in copies():
            copy.start()
        mine = col_ref[...] - start == lax.broadcasted_iota(jnp.int32, (GLOBALS, tok), 1)
        picked = dot(mine.astype(jnp.bfloat16), q_ref[...]) * DH ** (-0.5)
        for pair in range(PAIRS):
            lanes = slice(pair * LANES, (pair + 1) * LANES)
            gq[pair] = split_pair(picked[:, lanes]).astype(jnp.bfloat16)
        gk[...] = jnp.zeros_like(gk)
        gv[...] = jnp.zeros_like(gv)
        top[...] = jnp.full_like(top, -1e30)
        total[...] = jnp.zeros_like(total)
        acc[...] = jnp.zeros_like(acc)

    here = col_ref[...] - step * chunk == lax.broadcasted_iota(jnp.int32, (GLOBALS, chunk), 1)
    here = here.astype(jnp.bfloat16)
    gk[...] += dot(here, kc_ref[...])
    gv[...] += dot(here, vc_ref[...])
    for pair in range(PAIRS):
        lanes = slice(pair * LANES, (pair + 1) * LANES)
        scores = dot_t(gq[pair], kc_ref[:, lanes])
        before = top[pair]
        peak = jnp.maximum(before, jnp.max(scores, axis=1, keepdims=True))
        scale = jnp.exp(before - peak)
        terms = jnp.exp(scores - peak)
        top[pair] = peak
        total[pair] = total[pair] * scale + jnp.sum(terms, axis=1, keepdims=True)
        acc[pair] = acc[pair] * scale + dot(terms.astype(jnp.bfloat16), vc_ref[:, lanes])

    @pl.when(step == pl.num_programs(0) - 1)
    def _():
        for copy in copies():
            copy.wait()
        mine = row_ref[...] - start == lax.broadcasted_iota(jnp.int32, (tok, GLOBALS), 0)
        owned = jnp.max(jnp.where(mine, 1.0, 0.0), axis=1, keepdims=True) > 0.5
        mine = mine.astype(jnp.bfloat16)
        for pair in range(PAIRS):
            lanes = slice(pair * LANES, (pair + 1) * LANES)
            ratio = acc[pair] / total[pair]
            placed = join_pair(ratio[:GLOBALS], ratio[GLOBALS:]).astype(jnp.bfloat16)
            placed = dot(mine, placed)
            far_k = join_pair(dil_k[2 * pair], dil_k[2 * pair + 1])
            far_v = join_pair(dil_v[2 * pair], dil_v[2 * pair + 1])
            glob_k = gk[:, lanes].astype(jnp.bfloat16)
            glob_v = gv[:, lanes].astype(jnp.bfloat16)
            for block in range(tok // BLK):
                rows = slice(block * BLK, (block + 1) * BLK)
                near = slice(block * BLK, (block + 3) * BLK)
                keys = jnp.concatenate([loc_k[near, lanes], far_k[rows], glob_k], axis=0)
                values = jnp.concatenate([loc_v[near, lanes], far_v[rows], glob_v], axis=0)
                scores = dot_t(split_pair(q_ref[rows, lanes]), keys) * DH ** (-0.5)
                terms = jnp.exp(scores - jnp.max(scores, axis=1, keepdims=True))
                weights = terms * (1.0 / jnp.sum(terms, axis=1, keepdims=True))
                mixed = dot(weights.astype(jnp.bfloat16), values)
                mixed = join_pair(mixed[:BLK], mixed[BLK:])
                out_ref[rows, lanes] = jnp.where(owned[rows], placed[rows], mixed).astype(
                    jnp.bfloat16
                )


def attention(queries, keys, values, dilation, global_rows):
    tok, width = queries.shape
    length = keys.shape[0]
    me = lax.axis_index("seq").astype(jnp.int32)
    scal = jnp.concatenate([dilation, me[None]])
    whole = lambda shape: pl.BlockSpec(shape, lambda i, s: (0, 0))
    chunked = pl.BlockSpec((CHUNK, width), lambda i, s: (i, 0))
    raw = pl.BlockSpec(memory_space=pl.ANY)
    far = pltpu.VMEM((H, tok, LANES), jnp.bfloat16)
    near = pltpu.VMEM((tok + 2 * BLK, width), jnp.bfloat16)
    state = pltpu.VMEM((PAIRS, 2 * GLOBALS, 1), jnp.float32)
    return pl.pallas_call(
        functools.partial(attention_kernel, length),
        out_shape=jax.ShapeDtypeStruct((tok, width), jnp.bfloat16),
        grid_spec=pltpu.PrefetchScalarGridSpec(
            num_scalar_prefetch=1,
            grid=(length // CHUNK,),
            in_specs=[
                whole((tok, width)), whole((GLOBALS, 1)), whole((1, GLOBALS)),
                chunked, chunked, raw, raw,
            ],
            out_specs=whole((tok, width)),
            scratch_shapes=[
                near, near, far, far,
                pltpu.VMEM((PAIRS, 2 * GLOBALS, LANES), jnp.bfloat16),
                pltpu.VMEM((GLOBALS, width), jnp.float32),
                pltpu.VMEM((GLOBALS, width), jnp.float32),
                state, state,
                pltpu.VMEM((PAIRS, 2 * GLOBALS, LANES), jnp.float32),
                pltpu.SemaphoreType.DMA((2 * (H + 3),)),
            ],
        ),
        compiler_params=pltpu.CompilerParams(vmem_limit_bytes=40 << 20),
        cost_estimate=pl.CostEstimate(
            flops=20_000_000_000, bytes_accessed=4 * length * width, transcendentals=5_000_000
        ),
    )(scal, queries, global_rows[:, None], global_rows[None, :], keys, values, keys, values)


def per_device(queries, key_rows, value_rows, dilation, global_rows, out_weight, mlp_up, mlp_down):
    keys = lax.all_gather(key_rows, "seq", axis=0, tiled=True)
    values = lax.all_gather(value_rows, "seq", axis=0, tiled=True)
    keys, values, mlp_up, mlp_down = lax.optimization_barrier((keys, values, mlp_up, mlp_down))
    up = lax.all_gather(mlp_up, "seq", axis=0, tiled=True)
    down = lax.all_gather(mlp_down, "seq", axis=0, tiled=True)
    mixed = attention(queries, keys, values, dilation, global_rows)
    attended = jnp.dot(mixed, out_weight, preferred_element_type=jnp.float32).astype(jnp.bfloat16)
    pre_act = jnp.dot(attended, up, preferred_element_type=jnp.float32)
    hidden = jax.nn.gelu(pre_act, approximate=True).astype(jnp.bfloat16)
    mlp_out = jnp.dot(hidden, down, preferred_element_type=jnp.float32).astype(jnp.bfloat16)
    return attended, mlp_out


def solution(mesh):
    rows = P(("group", "seq"), None)
    return jax.shard_map(
        per_device,
        mesh=mesh,
        in_specs=(rows, rows, rows, P(), P("group"), P(), P("seq", None), P("seq", None)),
        out_specs=(rows, rows),
        check_vma=False,
    )
```

time: 400 us -> 321 us (0.80)
  waiting for transfers between devices: 104 us -> 261 us
  blocking collectives: 111 us -> 0 us
  local copies, waits for them, and re-layouts: 60.1 us -> 8.11 us
  other arithmetic: 50.4 us -> 0.73 us
  Pallas kernels: 0 us -> 23.1 us
  starting transfers between devices: 22.5 us -> 0.15 us
  matrix products: 34.8 us -> 13.2 us
    all_gather x3 -> x4, waiting for transfers between devices: 28 us -> 260 us  [the longest x1 81.7 us: per_device(): up = lax.all_gather(mlp_up, 'seq', axis=0, tiled=True)]
    ppermute x6 -> x0, waiting for transfers between devices: 74.8 us -> none  [the longest x4 74.8 us: passed_along(): return lax.ppermute(value, axis, pairs)]
    psum x1 -> x0, blocking collectives: 64.9 us -> none  [per_device(): glob_q, glob_k, glob_v = lax.psum((picked[0], picked[1], picked[2]), 'seq')]
    all_gather x2 -> x0, blocking collectives: 46.2 us -> none  [merged_2(): gathered = jax.tree.map(lambda a: lax.all_gather(a, axis), part)]
    add x30 -> x0, other arithmetic: 31.8 us -> none  [the longest x15 20.8 us: join_partials(): numer_first * scale_first[:, :, None]]
    pallas_call x0 -> x1, Pallas kernels: none -> 23.1 us  [attention(): pl.pallas_call(functools.partial(attention_kernel, length), out_shape=jax...]
    ppermute x6 -> x0, starting transfers between devices: 22.3 us -> none  [the longest x4 21.8 us: passed_along(): return lax.ppermute(value, axis, pairs)]
    reshape x9 -> x0, local copies, waits for them, and re-layouts: 18.3 us -> none  [the longest x4 10.9 us: select_heads(): arrived.reshape(shaped[0], shaped[1], H, DH)]
  transfers between devices with their start and end apart: 9 -> 4, of which waited for: 4 -> 4; matrix products, arithmetic and copies ran while one was open for 29% -> 1% of each run, Pallas kernels for 0% -> 7%
where the time goes in v1:
time: 321 us
  waiting for transfers between devices  261 us (81%)
  Pallas kernels  23.1 us (7%)
  between operations  13.8 us (4%)
  matrix products  13.2 us (4%)
  local copies, waits for them, and re-layouts  8.11 us (3%)
    all_gather x1, waiting for transfers between devices, per_device(): up = lax.all_gather(mlp_up, 'seq', axis=0, tiled=True)  81.7 us
    all_gather x1, waiting for transfers between devices, per_device(): keys = lax.all_gather(key_rows, 'seq', axis=0, tiled=True)  66 us
    all_gather x1, waiting for transfers between devices, per_device(): values = lax.all_gather(value_rows, 'seq', axis=0, tiled=True)  62.8 us
    all_gather x1, waiting for transfers between devices, per_device(): down = lax.all_gather(mlp_down, 'seq', axis=0, tiled=True)  49 us
    pallas_call x1, Pallas kernels, attention(): pl.pallas_call(functools.partial(attention_kernel, length), out_shape=jax...  23.1 us
    dot_general x1, matrix products, per_device(): jnp.dot(hidden, down, preferred_element_type=jnp.float32)  12.4 us
    unnamed x12, local copies, waits for them, and re-layouts  7.36 us
  transfers between devices with their start and end apart: 4, of which 4 were waited for; matrix products, arithmetic and copies ran while one was open for 1% of the time, Pallas kernels for 7%

profile of v1, /device:TPU:1, one launch (start us, length us, event | category | flops | bytes accessed | tf_op | source)
XLA Modules:
  0.0 320.5 jit_solution(5783202551212202289)
XLA Ops:
  7.2 0.0 copy-start
  7.2 0.0 all-gather.5.cloned.1.call-start
  7.2 0.7 all-gather.5.cloned.1.call-update
  7.9 0.0 all-gather.7.cloned.1.call-start
  8.0 0.7 all-gather.7.cloned.1.call-update
  8.7 0.0 all-gather.11.cloned.1.call-start
  8.7 66.0 %all-gather.5.cloned.1.call-done.kc_ref.k_hbm = bf16[4096,768]{1,0:T(8,128)(2,1)} async-done(((bf16[256,768]{1,0:T(8,128)(2,1)}), bf16[4096,768]{1,0:T(8,128)(2,1)}) %all-gather.5.cloned.1.call-update) | async-done | bytes 6291472 | tf_op jit(solution)/shard_map/all_gather | solution.py:173
  74.7 62.8 %all-gather.7.cloned.1.call-done.vc_ref.v_hbm = bf16[4096,768]{1,0:T(8,128)(2,1)} async-done(((bf16[256,768]{1,0:T(8,128)(2,1)}), bf16[4096,768]{1,0:T(8,128)(2,1)}) %all-gather.7.cloned.1.call-update) | async-done | bytes 6291472 | tf_op jit(solution)/shard_map/all_gather | solution.py:174
  137.4 0.0 all-gather.11.cloned.1.call-update
  137.5 0.0 all-gather.9.cloned.1.call-start
  137.5 0.5 all-gather.9.cloned.1.call-update
  138.1 0.7 copy.10.col_ref
  138.8 0.7 pad_add_fusion.scal
  139.5 0.0 copy-start.1
  139.5 0.7 copy-done.1
  140.2 0.0 copy-start.2
  140.2 2.8 copy-done.2
  143.0 0.0 copy-start.3
  143.0 2.9 copy-done.3
  145.8 0.0 copy-start.4
  145.8 1.0 copy-done.4
  146.9 23.1 %shard_map.95 = bf16[256,768]{1,0:T(8,128)(2,1)S(1)} custom-call(s32[13]{0:T(128)S(1)} %pad_add_fusion.scal, bf16[256,768]{1,0:T(8,128)(2,1)S(1)} %copy-done.4, s32[64,1]{1,0:T(8,128)S(1)} %copy.10.col_ref, s32[1,64]{1,0:T(1,128)S(1)} %bitcast.9, bf16[4096,768]{1,0:T(8,128)(2,1)S(1)} %copy-done.2, bf16[4096,768]{1,0:T(8,128)(2,1)S(1)} %copy-done.3, ...), custom_call_target="tpu_custom_call" | custom-call | flops 20000000000 | bytes 12582912 | tf_op jit(solution)/shard_map/pallas_call | solution.py:144
  170.0 0.0 copy-done
  170.0 0.8 convolution_convert_fusion.1
  170.8 0.0 copy-start.5
  170.8 49.0 %all-gather.11.cloned.1.call-done = bf16[3072,1536]{1,0:T(8,128)(2,1)} async-done(((bf16[192,1536]{1,0:T(8,128)(2,1)}), bf16[3072,1536]{1,0:T(8,128)(2,1)}) %all-gather.11.cloned.1.call-update) | async-done | bytes 9437200 | tf_op jit(solution)/shard_map/all_gather | solution.py:177
  219.8 81.7 %all-gather.9.cloned.1.call-done = bf16[1536,3072]{1,0:T(8,128)(2,1)} async-done(((bf16[96,3072]{1,0:T(8,128)(2,1)}), bf16[1536,3072]{1,0:T(8,128)(2,1)}) %all-gather.9.cloned.1.call-update) | async-done | bytes 9437200 | tf_op jit(solution)/shard_map/all_gather | solution.py:176
  301.6 12.4 %convolution_convert_fusion = bf16[256,1536]{1,0:T(8,128)(2,1)} fusion(bf16[3072,1536]{1,0:T(8,128)(2,1)} %all-gather.11.cloned.1.call-done, bf16[256,1536]{1,0:T(8,128)(2,1)S(1)} %convolution_convert_fusion.1, bf16[1536,3072]{1,0:T(8,128)(2,1)} %all-gather.9.cloned.1.call-done), kind=kOutput, calls=%fused_computation.9 | convolution fusion | flops 4839309312 | bytes 20447232 | tf_op jit(solution)/shard_map/dot_general | solution.py:182
  314.0 0.0 copy-done.5
Async XLA Ops:
  7.2 162.8 %copy-start = (bf16[768,1536]{1,0:T(8,128)(2,1)S(1)}, bf16[768,1536]{1,0:T(8,128)(2,1)}, u32[]{:S(2)}) copy-start(bf16[768,1536]{1,0:T(8,128)(2,1)} %param.13) | copy-start | bytes 7077892
  7.2 67.5 %all-gather.5.cloned.1.call-start = ((), (), s32[]{:S(2)}) async-start(), calls=%async_computation | async-start | bytes 6684672 | tf_op jit(solution)/shard_map/all_gather | solution.py:173
  7.9 129.5 %all-gather.7.cloned.1.call-start = ((), (), s32[]{:S(2)}) async-start(), calls=%async_computation.1 | async-start | bytes 6684672 | tf_op jit(solution)/shard_map/all_gather | solution.py:174
  8.7 211.2 %all-gather.11.cloned.1.call-start = ((), (), s32[]{:S(2)}) async-start(), calls=%async_computation.3 | async-start | bytes 10027008 | tf_op jit(solution)/shard_map/all_gather | solution.py:177
  137.5 164.1 %all-gather.9.cloned.1.call-start = ((), (), s32[]{:S(2)}) async-start(), calls=%async_computation.2 | async-start | bytes 10027008 | tf_op jit(solution)/shard_map/all_gather | solution.py:176
  139.5 0.7 copy-start.1
  140.2 2.8 copy-start.2
  143.0 2.9 copy-start.3
  145.8 1.0 copy-start.4
  170.8 143.2 %copy-start.5 = (bf16[256,1536]{1,0:T(8,128)(2,1)}, bf16[256,1536]{1,0:T(8,128)(2,1)S(1)}, u32[]{:S(2)}) copy-start(bf16[256,1536]{1,0:T(8,128)(2,1)S(1)} %convolution_convert_fusion.1) | copy-start | bytes 2359300
Sparse Core Ops, SparseCore 0:
  10.3 64.3 all-gather.4
  77.0 60.4 all-gather.6
  139.7 80.0 all-gather.10
  222.0 79.5 all-gather.8

commit v2 on v1

--- a/solution.py
+++ b/solution.py
@@ -169,12 +169,170 @@
     )(scal, queries, global_rows[:, None], global_rows[None, :], keys, values, keys, values)
 
 
+MESH = pl.DeviceIdType.MESH
+
+
+def gather_kernel(chips, *refs):
+    ins, outs, sems = refs[:4], refs[4:8], refs[8:]
+    ring_send, ring_recv, pair_send, pair_recv, core_send, core_recv, own_sems = sems
+    half = chips // 2
+    group, seq = lax.axis_index("group"), lax.axis_index("seq")
+    role = group % 2
+    chip, core = seq // 2, seq % 2
+    odd = chip % 2
+    pos = (1 - odd) * (chip // 2) + odd * (chips - 1 - chip // 2)
+
+    def chip_at(place):
+        place = (place + 2 * chips) % chips
+        late = place // half
+        return (1 - late) * 2 * place + late * (2 * (chips - 1 - place) + 1)
+
+    ahead = (group, chip_at(pos + 1) * 2 + core)
+    behind = (group, chip_at(pos - 1) * 2 + core)
+    beside = (group, chip * 2 + 1 - core)
+    across = (group + 1 - 2 * role, seq)
+
+    barrier = pltpu.get_barrier_semaphore()
+    for other in (ahead, behind, beside, across):
+        pl.semaphore_signal(barrier, inc=1, device_id=other, device_id_type=MESH)
+    pl.semaphore_wait(barrier, 4)
+
+    def columns(at, side, part):
+        width = ins[at].shape[1]
+        first = 0
+        if at < 2 and side is not None:
+            width = width // 2
+            first = side * width
+        if part is not None:
+            width = width // 2
+            first = first + part * width
+        if isinstance(first, int):
+            return pl.ds(first, width)
+        return pl.ds(pl.multiple_of(first, 128), width)
+
+    def held(at, place, side, part):
+        rows = ins[at].shape[0]
+        first = (chip_at(place) * 2 + core) * rows
+        return outs[at].at[pl.ds(pl.multiple_of(first, 8), rows), columns(at, side, part)]
+
+    def twin(at, place, side, part):
+        rows = ins[at].shape[0]
+        first = (chip_at(place) * 2 + 1 - core) * rows
+        return outs[at].at[pl.ds(pl.multiple_of(first, 8), rows), columns(at, side, part)]
+
+    def part_of(way, hop):
+        return way if hop == half else None
+
+    def sign(way):
+        return 1 - 2 * way
+
+    def remote(source, target, send, recv, other):
+        return pltpu.make_async_remote_copy(
+            src_ref=source, dst_ref=target, send_sem=send, recv_sem=recv,
+            device_id=other, device_id_type=MESH,
+        )
+
+    sent = []
+
+    def ring(at, way, hop):
+        index = (at * 2 + way) * half + hop - 1
+        return ring_send.at[index], ring_recv.at[index], (ahead, behind)[way]
+
+    def ring_start(at, way, hop):
+        place, part = pos - sign(way) * (hop - 1), part_of(way, hop)
+        target = held(at, place, role, part)
+        source = ins[at].at[:, columns(at, role, part)] if hop == 1 else target
+        copy = remote(source, target, *ring(at, way, hop))
+        copy.start()
+        sent.append(copy)
+
+    def ring_wait(at, way, hop):
+        here = held(at, pos - sign(way) * hop, role, part_of(way, hop))
+        remote(here, here, *ring(at, way, hop)).wait_recv()
+
+    def pair(at, way, hop):
+        index = (at * 2 + way) * half + hop - 1
+        return pair_send.at[index], pair_recv.at[index], across
+
+    def pair_start(at, way, hop):
+        here = held(at, pos - sign(way) * hop, role, part_of(way, hop))
+        copy = remote(here, here, *pair(at, way, hop))
+        copy.start()
+        sent.append(copy)
+
+    def pair_wait(at, way, hop):
+        here = held(at, pos - sign(way) * hop, 1 - role, part_of(way, hop))
+        remote(here, here, *pair(at, way, hop)).wait_recv()
+
+    passed = []
+
+    def core_start(at, place, side, part, source=None):
+        index = len(passed)
+        target = held(at, place, side, part)
+        copy = remote(
+            target if source is None else source, target,
+            core_send.at[index], core_recv.at[index], beside,
+        )
+        copy.start()
+        sent.append(copy)
+        passed.append((at, place, side, part))
+
+    own = []
+    for at in range(4):
+        for way in range(2):
+            ring_start(at, way, 1)
+    for at in range(4):
+        core_start(at, pos, None, None, ins[at])
+        copy = pltpu.make_async_copy(ins[at], held(at, pos, None, None), own_sems.at[at])
+        copy.start()
+        own.append(copy)
+    for hop in range(1, half + 2):
+        if hop <= half:
+            for at in range(4):
+                for way in range(2):
+                    ring_wait(at, way, hop)
+                    if hop < half:
+                        ring_start(at, way, hop + 1)
+                    if at < 2:
+                        pair_start(at, way, hop)
+                    core_start(at, pos - sign(way) * hop, role, part_of(way, hop))
+        if hop > 1:
+            for at in range(2):
+                for way in range(2):
+                    pair_wait(at, way, hop - 1)
+                    core_start(at, pos - sign(way) * (hop - 1), 1 - role, part_of(way, hop - 1))
+    for index, (at, place, side, part) in enumerate(passed):
+        here = twin(at, place, side, part)
+        remote(here, here, core_send.at[index], core_recv.at[index], beside).wait_recv()
+    for copy in sent:
+        copy.wait_send()
+    for copy in own:
+        copy.wait()
+
+
+def gathered(arrays):
+    devices = lax.axis_size("seq")
+    chips = devices // 2
+    half = chips // 2
+    raw = pl.BlockSpec(memory_space=pl.ANY)
+    dma = pltpu.SemaphoreType.DMA
+    return pl.pallas_call(
+        functools.partial(gather_kernel, chips),
+        out_shape=[
+            jax.ShapeDtypeStruct((a.shape[0] * devices, a.shape[1]), a.dtype) for a in arrays
+        ],
+        in_specs=[raw] * 4,
+        out_specs=[raw] * 4,
+        scratch_shapes=[
+            dma((8 * half,)), dma((8 * half,)), dma((4 * half,)), dma((4 * half,)),
+            dma((4 + 12 * half,)), dma((4 + 12 * half,)), dma((4,)),
+        ],
+        compiler_params=pltpu.CompilerParams(collective_id=0, has_side_effects=True),
+    )(*arrays)
+
+
 def per_device(queries, key_rows, value_rows, dilation, global_rows, out_weight, mlp_up, mlp_down):
-    keys = lax.all_gather(key_rows, "seq", axis=0, tiled=True)
-    values = lax.all_gather(value_rows, "seq", axis=0, tiled=True)
-    keys, values, mlp_up, mlp_down = lax.optimization_barrier((keys, values, mlp_up, mlp_down))
-    up = lax.all_gather(mlp_up, "seq", axis=0, tiled=True)
-    down = lax.all_gather(mlp_down, "seq", axis=0, tiled=True)
+    up, down, keys, values = gathered((mlp_up, mlp_down, key_rows, value_rows))
     mixed = attention(queries, keys, values, dilation, global_rows)
     attended = jnp.dot(mixed, out_weight, preferred_element_type=jnp.float32).astype(jnp.bfloat16)
     pre_act = jnp.dot(attended, up, preferred_element_type=jnp.float32)

time: 321 us -> 161 us (0.50)
  waiting for transfers between devices: 261 us -> 0 us
  Pallas kernels: 23.1 us -> 138 us
  between operations: 13.8 us -> 0.69 us
    all_gather x4 -> x0, waiting for transfers between devices: 260 us -> none  [the longest x1 81.7 us: per_device(): up = lax.all_gather(mlp_up, 'seq', axis=0, tiled=True)]
    pallas_call x0 -> x1, Pallas kernels: none -> 115 us  [gathered(): pl.pallas_call(functools.partial(gather_kernel, chips), out_shape=[jax.Sh...]
  transfers between devices with their start and end apart: 4 -> 0, of which waited for: 4 -> 0; matrix products, arithmetic and copies ran while one was open for 1% -> 0% of each run, Pallas kernels for 7% -> 0%
where the time goes in v2:
time: 161 us
  Pallas kernels  138 us (86%)
  matrix products  13.5 us (8%)
  local copies, waits for them, and re-layouts  7.97 us (5%)
    pallas_call x1, Pallas kernels, gathered(): pl.pallas_call(functools.partial(gather_kernel, chips), out_shape=[jax.Sh...  115 us
    pallas_call x1, Pallas kernels, attention(): pl.pallas_call(functools.partial(attention_kernel, length), out_shape=jax...  22.9 us
    dot_general x1, matrix products, per_device(): jnp.dot(hidden, down, preferred_element_type=jnp.float32)  12.7 us
    unnamed x12, local copies, waits for them, and re-layouts  7.23 us

profile of v2, /device:TPU:1, one launch (start us, length us, event | category | flops | bytes accessed | tf_op | source)
XLA Modules:
  0.0 160.6 jit_solution(13649942926179202924)
XLA Ops:
  0.6 0.0 copy-start
  0.6 0.9 pad_add_fusion.scal
  1.5 0.7 copy.10.col_ref
  2.3 114.7 %shard_map.95 = (bf16[1536,3072]{1,0:T(8,128)(2,1)}, bf16[3072,1536]{1,0:T(8,128)(2,1)}, bf16[4096,768]{1,0:T(8,128)(2,1)}, bf16[4096,768]{1,0:T(8,128)(2,1)}) custom-call(bf16[96,3072]{1,0:T(8,128)(2,1)} %refs_0_.1, bf16[192,1536]{1,0:T(8,128)(2,1)} %refs_1_.1, bf16[256,768]{1,0:T(8,128)(2,1)} %refs_2_.1, bf16[256,768]{1,0:T(8,128)(2,1)} %refs_3_.1), custom_call_target="tpu_custom_call" | custom-call | tf_op jit(solution)/shard_map/pallas_call | solution.py:319
  116.9 0.0 copy-start.1
  117.0 0.6 copy-done.1
  117.6 0.0 copy-start.2
  117.6 2.8 %copy-done.2 = bf16[4096,768]{1,0:T(8,128)(2,1)S(1)} copy-done((bf16[4096,768]{1,0:T(8,128)(2,1)S(1)}, bf16[4096,768]{1,0:T(8,128)(2,1)}, u32[]{:S(2)}) %copy-start.2) | copy-done | bytes 6291480
  120.4 0.0 copy-start.3
  120.4 2.8 %copy-done.3 = bf16[4096,768]{1,0:T(8,128)(2,1)S(1)} copy-done((bf16[4096,768]{1,0:T(8,128)(2,1)S(1)}, bf16[4096,768]{1,0:T(8,128)(2,1)}, u32[]{:S(2)}) %copy-start.3) | copy-done | bytes 6291480
  123.2 0.0 copy-start.4
  123.2 1.0 copy-done.4
  124.2 22.9 %shard_map.96 = bf16[256,768]{1,0:T(8,128)(2,1)S(1)} custom-call(s32[13]{0:T(128)S(1)} %pad_add_fusion.scal, bf16[256,768]{1,0:T(8,128)(2,1)S(1)} %copy-done.4, s32[64,1]{1,0:T(8,128)S(1)} %copy.10.col_ref, s32[1,64]{1,0:T(1,128)S(1)} %bitcast.9, bf16[4096,768]{1,0:T(8,128)(2,1)S(1)} %copy-done.2, bf16[4096,768]{1,0:T(8,128)(2,1)S(1)} %copy-done.3, ...), custom_call_target="tpu_custom_call" | custom-call | flops 20000000000 | bytes 12582912 | tf_op jit(solution)/shard_map/pallas_call | solution.py:144
  147.1 0.0 copy-done
  147.1 0.8 convolution_convert_fusion.1
  147.8 0.0 copy-start.5
  147.9 12.7 %convolution_convert_fusion = bf16[256,1536]{1,0:T(8,128)(2,1)} fusion(bf16[3072,1536]{1,0:T(8,128)(2,1)} %get-tuple-element.9, bf16[256,1536]{1,0:T(8,128)(2,1)S(1)} %convolution_convert_fusion.1, bf16[1536,3072]{1,0:T(8,128)(2,1)} %get-tuple-element.8), kind=kOutput, calls=%fused_computation.9 | convolution fusion | flops 4839309312 | bytes 20447232 | tf_op jit(solution)/shard_map/dot_general | solution.py:340
  160.6 0.0 copy-done.5
Async XLA Ops:
  0.6 146.4 %copy-start = (bf16[768,1536]{1,0:T(8,128)(2,1)S(1)}, bf16[768,1536]{1,0:T(8,128)(2,1)}, u32[]{:S(2)}) copy-start(bf16[768,1536]{1,0:T(8,128)(2,1)} %param.13) | copy-start | bytes 7077892
  116.9 0.7 copy-start.1
  117.6 2.8 %copy-start.2 = (bf16[4096,768]{1,0:T(8,128)(2,1)S(1)}, bf16[4096,768]{1,0:T(8,128)(2,1)}, u32[]{:S(2)}) copy-start(bf16[4096,768]{1,0:T(8,128)(2,1)} %get-tuple-element.6.kc_ref.k_hbm) | copy-start | bytes 18874372
  120.4 2.8 %copy-start.3 = (bf16[4096,768]{1,0:T(8,128)(2,1)S(1)}, bf16[4096,768]{1,0:T(8,128)(2,1)}, u32[]{:S(2)}) copy-start(bf16[4096,768]{1,0:T(8,128)(2,1)} %get-tuple-element.7.vc_ref.v_hbm) | copy-start | bytes 18874372
  123.2 1.0 copy-start.4
  147.8 12.7 %copy-start.5 = (bf16[256,1536]{1,0:T(8,128)(2,1)}, bf16[256,1536]{1,0:T(8,128)(2,1)S(1)}, u32[]{:S(2)}) copy-start(bf16[256,1536]{1,0:T(8,128)(2,1)S(1)} %convolution_convert_fusion.1) | copy-start | bytes 2359300

commit v3 on v2

--- a/solution.py
+++ b/solution.py
@@ -14,6 +14,8 @@
 LANES = 2 * DH
 PAIRS = H // 2
 CHUNK = 1024
+SLOTS = 16
+TILE = 16
 
 
 def split_pair(rows):
@@ -39,14 +41,19 @@
     return jnp.dot(left, right, preferred_element_type=jnp.float32)
 
 
+def head_mask(shape):
+    row = lax.broadcasted_iota(jnp.int32, shape, 0) // SLOTS
+    lane = lax.broadcasted_iota(jnp.int32, shape, 1) // DH
+    return row == lane
+
+
 def attention_kernel(
     length, scal, q_ref, col_ref, row_ref, kc_ref, vc_ref, k_hbm, v_hbm, out_ref,
-    loc_k, loc_v, dil_k, dil_v, gq, gk, gv, top, total, acc, sems,
+    loc_k, loc_v, dil_k, dil_v, tile_k, tile_v, gq, top, total, acc, sems,
 ):
     step = pl.program_id(0)
-    tok = q_ref.shape[0]
-    chunk = kc_ref.shape[0]
-    me = scal[H]
+    tok, width = q_ref.shape
+    me, count = scal[H], scal[H + 1]
     start = me * tok
 
     def copies():
@@ -69,52 +76,92 @@
             for at, (source, target) in enumerate(made)
         ]
 
+    def slots():
+        rows, cols = row_ref[...] - start, col_ref[...] - start
+        row_own = jnp.where((rows >= 0) & (rows < tok), 1.0, 0.0)
+        col_own = jnp.where((cols >= 0) & (cols < tok), 1.0, 0.0)
+        square = (GLOBALS, GLOBALS)
+        down = lax.broadcasted_iota(jnp.int32, square, 0)
+        right = lax.broadcasted_iota(jnp.int32, square, 1)
+        return rows, cols, row_own, col_own, down, right
+
+    def picker_rows(group):
+        rows, cols, row_own, col_own, down, right = slots()
+        rank = jnp.sum(jnp.where(down < right, col_own, 0.0), axis=0, keepdims=True)
+        rank = jnp.where(row_own > 0.5, rank, -1.0).astype(jnp.int32)
+        slot = lax.broadcasted_iota(jnp.int32, (H * SLOTS, GLOBALS), 0) % SLOTS
+        holds = jnp.where(slot + group * SLOTS == rank, 1.0, 0.0).astype(jnp.bfloat16)
+        at = jnp.where(
+            cols == lax.broadcasted_iota(jnp.int32, (GLOBALS, tok), 1), 1.0, 0.0
+        ).astype(jnp.bfloat16)
+        return dot(holds, at).astype(jnp.bfloat16)
+
+    def picker_cols(group):
+        rows, cols, row_own, col_own, down, right = slots()
+        rank = jnp.sum(jnp.where(right < down, row_own, 0.0), axis=1, keepdims=True)
+        rank = jnp.where(col_own > 0.5, rank, -1.0).astype(jnp.int32)
+        slot = lax.broadcasted_iota(jnp.int32, (GLOBALS, H * SLOTS), 1) % SLOTS
+        holds = jnp.where(slot + group * SLOTS == rank, 1.0, 0.0).astype(jnp.bfloat16)
+        at = jnp.where(
+            rows == lax.broadcasted_iota(jnp.int32, (tok, GLOBALS), 0), 1.0, 0.0
+        ).astype(jnp.bfloat16)
+        return dot(at, holds).astype(jnp.bfloat16)
+
     @pl.when(step == 0)
     def _():
         for copy in copies():
             copy.start()
-        mine = col_ref[...] - start == lax.broadcasted_iota(jnp.int32, (GLOBALS, tok), 1)
-        picked = dot(mine.astype(jnp.bfloat16), q_ref[...]) * DH ** (-0.5)
-        for pair in range(PAIRS):
-            lanes = slice(pair * LANES, (pair + 1) * LANES)
-            gq[pair] = split_pair(picked[:, lanes]).astype(jnp.bfloat16)
-        gk[...] = jnp.zeros_like(gk)
-        gv[...] = jnp.zeros_like(gv)
-        top[...] = jnp.full_like(top, -1e30)
-        total[...] = jnp.zeros_like(total)
-        acc[...] = jnp.zeros_like(acc)
-
-    here = col_ref[...] - step * chunk == lax.broadcasted_iota(jnp.int32, (GLOBALS, chunk), 1)
-    here = here.astype(jnp.bfloat16)
-    gk[...] += dot(here, kc_ref[...])
-    gv[...] += dot(here, vc_ref[...])
-    for pair in range(PAIRS):
-        lanes = slice(pair * LANES, (pair + 1) * LANES)
-        scores = dot_t(gq[pair], kc_ref[:, lanes])
-        before = top[pair]
-        peak = jnp.maximum(before, jnp.max(scores, axis=1, keepdims=True))
-        scale = jnp.exp(before - peak)
-        terms = jnp.exp(scores - peak)
-        top[pair] = peak
-        total[pair] = total[pair] * scale + jnp.sum(terms, axis=1, keepdims=True)
-        acc[pair] = acc[pair] * scale + dot(terms.astype(jnp.bfloat16), vc_ref[:, lanes])
+
+        @pl.loop(0, GLOBALS)
+        def _(at):
+            source = pl.ds(pl.multiple_of(scal[H + 2 + at] // TILE * TILE, TILE), TILE)
+            target = pl.ds(pl.multiple_of(at * TILE, TILE), TILE)
+            for index, (hbm, tile) in enumerate(((k_hbm, tile_k), (v_hbm, tile_v))):
+                pltpu.make_async_copy(
+                    hbm.at[source, :], tile.at[target, :], sems.at[2 * (H + 3) + index]
+                ).start()
+
+        for group in range(GLOBALS // SLOTS):
+
+            @pl.when(count > group * SLOTS)
+            def _():
+                picked = dot(picker_rows(group), q_ref[...]) * DH ** (-0.5)
+                picked = jnp.where(head_mask(picked.shape), picked, 0.0)
+                gq[group] = picked.astype(jnp.bfloat16)
+                top[group] = jnp.full(top.shape[1:], -1e30, jnp.float32)
+                total[group] = jnp.zeros(total.shape[1:], jnp.float32)
+                acc[group] = jnp.zeros(acc.shape[1:], jnp.float32)
+
+    for group in range(GLOBALS // SLOTS):
+
+        @pl.when(count > group * SLOTS)
+        def _():
+            scores = dot_t(gq[group], kc_ref[...])
+            before = top[group]
+            peak = jnp.maximum(before, jnp.max(scores, axis=1, keepdims=True))
+            scale = jnp.exp(before - peak)
+            terms = jnp.exp(scores - peak)
+            top[group] = peak
+            total[group] = total[group] * scale + jnp.sum(terms, axis=1, keepdims=True)
+            acc[group] = acc[group] * scale + dot(terms.astype(jnp.bfloat16), vc_ref[...])
 
     @pl.when(step == pl.num_programs(0) - 1)
     def _():
         for copy in copies():
             copy.wait()
-        mine = row_ref[...] - start == lax.broadcasted_iota(jnp.int32, (tok, GLOBALS), 0)
-        owned = jnp.max(jnp.where(mine, 1.0, 0.0), axis=1, keepdims=True) > 0.5
-        mine = mine.astype(jnp.bfloat16)
+        for index, (hbm, tile) in enumerate(((k_hbm, tile_k), (v_hbm, tile_v))):
+            pltpu.make_async_copy(
+                hbm.at[pl.ds(0, GLOBALS * TILE), :], tile, sems.at[2 * (H + 3) + index]
+            ).wait()
+        spot = lax.broadcasted_iota(jnp.int32, (GLOBALS, GLOBALS * TILE), 1)
+        want = lax.broadcasted_iota(jnp.int32, (GLOBALS, GLOBALS * TILE), 0) * TILE
+        here = jnp.where(spot == want + col_ref[...] % TILE, 1.0, 0.0).astype(jnp.bfloat16)
         for pair in range(PAIRS):
             lanes = slice(pair * LANES, (pair + 1) * LANES)
-            ratio = acc[pair] / total[pair]
-            placed = join_pair(ratio[:GLOBALS], ratio[GLOBALS:]).astype(jnp.bfloat16)
-            placed = dot(mine, placed)
             far_k = join_pair(dil_k[2 * pair], dil_k[2 * pair + 1])
             far_v = join_pair(dil_v[2 * pair], dil_v[2 * pair + 1])
-            glob_k = gk[:, lanes].astype(jnp.bfloat16)
-            glob_v = gv[:, lanes].astype(jnp.bfloat16)
+            glob_k = dot(here, tile_k[:, lanes]).astype(jnp.bfloat16)
+            glob_v = dot(here, tile_v[:, lanes]).astype(jnp.bfloat16)
             for block in range(tok // BLK):
                 rows = slice(block * BLK, (block + 1) * BLK)
                 near = slice(block * BLK, (block + 3) * BLK)
@@ -125,22 +172,34 @@
                 weights = terms * (1.0 / jnp.sum(terms, axis=1, keepdims=True))
                 mixed = dot(weights.astype(jnp.bfloat16), values)
                 mixed = join_pair(mixed[:BLK], mixed[BLK:])
-                out_ref[rows, lanes] = jnp.where(owned[rows], placed[rows], mixed).astype(
-                    jnp.bfloat16
-                )
+                out_ref[rows, lanes] = mixed.astype(jnp.bfloat16)
+
+        for group in range(GLOBALS // SLOTS):
+
+            @pl.when(count > group * SLOTS)
+            def _():
+                ratio = acc[group] / total[group]
+                ratio = jnp.where(head_mask(ratio.shape), ratio, 0.0).astype(jnp.bfloat16)
+                mine = picker_cols(group)
+                placed = dot(mine, ratio).astype(jnp.bfloat16)
+                owned = jnp.max(mine.astype(jnp.float32), axis=1, keepdims=True) > 0.5
+                out_ref[...] = jnp.where(owned, placed, out_ref[...])
 
 
 def attention(queries, keys, values, dilation, global_rows):
     tok, width = queries.shape
     length = keys.shape[0]
+    groups = GLOBALS // SLOTS
     me = lax.axis_index("seq").astype(jnp.int32)
-    scal = jnp.concatenate([dilation, me[None]])
+    count = jnp.sum((global_rows // tok == me).astype(jnp.int32))
+    scal = jnp.concatenate([dilation, me[None], count[None], global_rows])
     whole = lambda shape: pl.BlockSpec(shape, lambda i, s: (0, 0))
     chunked = pl.BlockSpec((CHUNK, width), lambda i, s: (i, 0))
     raw = pl.BlockSpec(memory_space=pl.ANY)
     far = pltpu.VMEM((H, tok, LANES), jnp.bfloat16)
     near = pltpu.VMEM((tok + 2 * BLK, width), jnp.bfloat16)
-    state = pltpu.VMEM((PAIRS, 2 * GLOBALS, 1), jnp.float32)
+    tile = pltpu.VMEM((GLOBALS * TILE, width), jnp.bfloat16)
+    state = pltpu.VMEM((groups, H * SLOTS, 1), jnp.float32)
     return pl.pallas_call(
         functools.partial(attention_kernel, length),
         out_shape=jax.ShapeDtypeStruct((tok, width), jnp.bfloat16),
@@ -153,16 +212,14 @@
             ],
             out_specs=whole((tok, width)),
             scratch_shapes=[
-                near, near, far, far,
-                pltpu.VMEM((PAIRS, 2 * GLOBALS, LANES), jnp.bfloat16),
-                pltpu.VMEM((GLOBALS, width), jnp.float32),
-                pltpu.VMEM((GLOBALS, width), jnp.float32),
+                near, near, far, far, tile, tile,
+                pltpu.VMEM((groups, H * SLOTS, width), jnp.bfloat16),
                 state, state,
-                pltpu.VMEM((PAIRS, 2 * GLOBALS, LANES), jnp.float32),
-                pltpu.SemaphoreType.DMA((2 * (H + 3),)),
+                pltpu.VMEM((groups, H * SLOTS, width), jnp.float32),
+                pltpu.SemaphoreType.DMA((2 * (H + 3) + 2,)),
             ],
         ),
-        compiler_params=pltpu.CompilerParams(vmem_limit_bytes=40 << 20),
+        compiler_params=pltpu.CompilerParams(vmem_limit_bytes=58 << 20),
         cost_estimate=pl.CostEstimate(
             flops=20_000_000_000, bytes_accessed=4 * length * width, transcendentals=5_000_000
         ),
@@ -278,7 +335,10 @@
         passed.append((at, place, side, part))
 
     own = []
-    for at in range(4):
+    for at in (0, 1):
+        for way in range(2):
+            ring_start(at, way, 1)
+    for at in (2, 3):
         for way in range(2):
             ring_start(at, way, 1)
     for at in range(4):
@@ -286,17 +346,23 @@
         copy = pltpu.make_async_copy(ins[at], held(at, pos, None, None), own_sems.at[at])
         copy.start()
         own.append(copy)
+
+    def ring_step(at, hop):
+        for way in range(2):
+            ring_wait(at, way, hop)
+            if hop < half:
+                ring_start(at, way, hop + 1)
+            if at < 2:
+                pair_start(at, way, hop)
+            core_start(at, pos - sign(way) * hop, role, part_of(way, hop))
+
     for hop in range(1, half + 2):
         if hop <= half:
-            for at in range(4):
-                for way in range(2):
-                    ring_wait(at, way, hop)
-                    if hop < half:
-                        ring_start(at, way, hop + 1)
-                    if at < 2:
-                        pair_start(at, way, hop)
-                    core_start(at, pos - sign(way) * hop, role, part_of(way, hop))
+            ring_step(0, hop)
+            ring_step(1, hop)
         if hop > 1:
+            ring_step(2, hop - 1)
+            ring_step(3, hop - 1)
             for at in range(2):
                 for way in range(2):
                     pair_wait(at, way, hop - 1)

time: 161 us -> 153 us (0.950)
  local copies, waits for them, and re-layouts: 7.97 us -> 1.37 us
  Pallas kernels: 138 us -> 133 us
  other arithmetic: 0.88 us -> 3.42 us
    unnamed x12 -> x4, local copies, waits for them, and re-layouts: 7.23 us -> 0.02 us
    pallas_call x1, Pallas kernels: 22.9 us -> 19.6 us  [attention(): pl.pallas_call(functools.partial(attention_kernel, length), out_shape=jax...]
    pallas_call x1, Pallas kernels: 115 us -> 113 us  [gathered(): pl.pallas_call(functools.partial(gather_kernel, chips), out_shape=[jax.Sh...]
where the time goes in v3:
time: 153 us; the launch traced here: 152 us
  Pallas kernels  133 us (87%)
  matrix products  14.5 us (9%)
  other arithmetic  3.42 us (2%)
    pallas_call x1, Pallas kernels, gathered(): pl.pallas_call(functools.partial(gather_kernel, chips), out_shape=[jax.Sh...  113 us
    pallas_call x1, Pallas kernels, attention(): pl.pallas_call(functools.partial(attention_kernel, length), out_shape=jax...  19.6 us
    dot_general x1, matrix products, per_device(): jnp.dot(hidden, down, preferred_element_type=jnp.float32)  12.7 us

profile of v3, /device:TPU:1, one launch (start us, length us, event | category | flops | bytes accessed | tf_op | source)
XLA Modules:
  0.0 152.5 jit_solution(3811927854977963019)
XLA Ops:
  0.6 0.0 copy-start
  0.6 1.5 fusion.13
  2.1 2.0 %pad_add_fusion.scal = s32[78]{0:T(128)} fusion(s32[64]{0:T(128)} %param.12, s32[1]{0:T(128)} %bitcast.1, s32[1]{0:T(128)} %bitcast, s32[12]{0:T(128)} %param.11), kind=kLoop, calls=%fused_computation.21 | loop fusion | flops 234 | bytes 624 | tf_op jit(solution)/shard_map/concatenate | solution.py:195
  4.1 1.4 copy.10.col_ref
  5.4 112.9 %shard_map.95 = (bf16[1536,3072]{1,0:T(8,128)(2,1)}, bf16[3072,1536]{1,0:T(8,128)(2,1)}, bf16[4096,768]{1,0:T(8,128)(2,1)}, bf16[4096,768]{1,0:T(8,128)(2,1)}) custom-call(bf16[96,3072]{1,0:T(8,128)(2,1)} %refs_0_.1, bf16[192,1536]{1,0:T(8,128)(2,1)} %refs_1_.1, bf16[256,768]{1,0:T(8,128)(2,1)} %refs_2_.1, bf16[256,768]{1,0:T(8,128)(2,1)} %refs_3_.1), custom_call_target="tpu_custom_call" | custom-call | tf_op jit(solution)/shard_map/pallas_call | solution.py:385
  118.4 19.6 %shard_map.96 = bf16[256,768]{1,0:T(8,128)(2,1)} custom-call(s32[78]{0:T(128)} %pad_add_fusion.scal, bf16[256,768]{1,0:T(8,128)(2,1)} %q_ref.1, s32[64,1]{1,0:T(8,128)} %copy.10.col_ref, s32[1,64]{1,0:T(1,128)} %bitcast.10, bf16[4096,768]{1,0:T(8,128)(2,1)} %get-tuple-element.6.kc_ref.k_hbm, bf16[4096,768]{1,0:T(8,128)(2,1)} %get-tuple-element.7.vc_ref.v_hbm, ...), custom_call_target="tpu_custom_call" | custom-call | flops 20000000000 | bytes 12582912 | tf_op jit(solution)/shard_map/pallas_call | solution.py:203
  137.9 0.0 copy-done
  138.0 1.8 %convolution_convert_fusion.1 = bf16[256,1536]{1,0:T(8,128)(2,1)S(1)} fusion(bf16[256,768]{1,0:T(8,128)(2,1)} %shard_map.96, bf16[768,1536]{1,0:T(8,128)(2,1)S(1)} %copy-done), kind=kOutput, calls=%fused_computation.10 | convolution fusion | flops 604372992 | bytes 3538944 | tf_op jit(solution)/shard_map/dot_general | solution.py:403
  139.7 0.0 copy-start.1
  139.7 12.7 %convolution_convert_fusion = bf16[256,1536]{1,0:T(8,128)(2,1)} fusion(bf16[3072,1536]{1,0:T(8,128)(2,1)} %get-tuple-element.9, bf16[256,1536]{1,0:T(8,128)(2,1)S(1)} %convolution_convert_fusion.1, bf16[1536,3072]{1,0:T(8,128)(2,1)} %get-tuple-element.8), kind=kOutput, calls=%fused_computation.9 | convolution fusion | flops 4839309312 | bytes 20447232 | tf_op jit(solution)/shard_map/dot_general | solution.py:406
  152.5 0.0 copy-done.1
Async XLA Ops:
  0.6 137.3 %copy-start = (bf16[768,1536]{1,0:T(8,128)(2,1)S(1)}, bf16[768,1536]{1,0:T(8,128)(2,1)}, u32[]{:S(2)}) copy-start(bf16[768,1536]{1,0:T(8,128)(2,1)} %param.13) | copy-start | bytes 7077892
  139.7 12.7 %copy-start.1 = (bf16[256,1536]{1,0:T(8,128)(2,1)}, bf16[256,1536]{1,0:T(8,128)(2,1)S(1)}, u32[]{:S(2)}) copy-start(bf16[256,1536]{1,0:T(8,128)(2,1)S(1)} %convolution_convert_fusion.1) | copy-start | bytes 2359300

commit v4 on v3

--- a/solution.py
+++ b/solution.py
@@ -48,12 +48,12 @@
 
 
 def attention_kernel(
-    length, scal, q_ref, col_ref, row_ref, kc_ref, vc_ref, k_hbm, v_hbm, out_ref,
-    loc_k, loc_v, dil_k, dil_v, tile_k, tile_v, gq, top, total, acc, sems,
+    length, dilation, spots, q_ref, row_ref, kc_ref, vc_ref, k_hbm, v_hbm, out_ref,
+    loc_k, loc_v, dil_k, dil_v, tile_k, tile_v, gq, top, total, acc, owns, sems,
 ):
     step = pl.program_id(0)
     tok, width = q_ref.shape
-    me, count = scal[H], scal[H + 1]
+    me = lax.axis_index("seq")
     start = me * tok
 
     def copies():
@@ -68,7 +68,7 @@
                 rows = pl.ds(pl.multiple_of(source, BLK), size)
                 made.append((hbm.at[rows, :], loc.at[pl.ds(target, size), :]))
             for head in range(H):
-                source = lax.rem(start + scal[head] * BLK, length)
+                source = lax.rem(start + dilation[head] * BLK, length)
                 rows = pl.ds(pl.multiple_of(source, BLK), tok)
                 made.append((hbm.at[rows, pl.ds(head // 2 * LANES, LANES)], dil.at[head]))
         return [
@@ -76,8 +76,15 @@
             for at, (source, target) in enumerate(made)
         ]
 
+    def column():
+        square = (GLOBALS, GLOBALS)
+        down = lax.broadcasted_iota(jnp.int32, square, 0)
+        right = lax.broadcasted_iota(jnp.int32, square, 1)
+        spread = jnp.where(down == right, row_ref[...].astype(jnp.float32), 0.0)
+        return jnp.sum(spread, axis=1, keepdims=True).astype(jnp.int32)
+
     def slots():
-        rows, cols = row_ref[...] - start, col_ref[...] - start
+        rows, cols = row_ref[...] - start, column() - start
         row_own = jnp.where((rows >= 0) & (rows < tok), 1.0, 0.0)
         col_own = jnp.where((cols >= 0) & (cols < tok), 1.0, 0.0)
         square = (GLOBALS, GLOBALS)
@@ -112,18 +119,20 @@
         for copy in copies():
             copy.start()
 
-        @pl.loop(0, GLOBALS)
-        def _(at):
-            source = pl.ds(pl.multiple_of(scal[H + 2 + at] // TILE * TILE, TILE), TILE)
+        def fetch(at, count):
+            spot = spots[at]
+            source = pl.ds(pl.multiple_of(spot // TILE * TILE, TILE), TILE)
             target = pl.ds(pl.multiple_of(at * TILE, TILE), TILE)
             for index, (hbm, tile) in enumerate(((k_hbm, tile_k), (v_hbm, tile_v))):
                 pltpu.make_async_copy(
                     hbm.at[source, :], tile.at[target, :], sems.at[2 * (H + 3) + index]
                 ).start()
-
+            return count + jnp.where(spot // tok == me, 1, 0)
+
+        owns[0] = lax.fori_loop(0, GLOBALS, fetch, jnp.int32(0))
         for group in range(GLOBALS // SLOTS):
 
-            @pl.when(count > group * SLOTS)
+            @pl.when(owns[0] > group * SLOTS)
             def _():
                 picked = dot(picker_rows(group), q_ref[...]) * DH ** (-0.5)
                 picked = jnp.where(head_mask(picked.shape), picked, 0.0)
@@ -134,7 +143,7 @@
 
     for group in range(GLOBALS // SLOTS):
 
-        @pl.when(count > group * SLOTS)
+        @pl.when(owns[0] > group * SLOTS)
         def _():
             scores = dot_t(gq[group], kc_ref[...])
             before = top[group]
@@ -155,7 +164,7 @@
             ).wait()
         spot = lax.broadcasted_iota(jnp.int32, (GLOBALS, GLOBALS * TILE), 1)
         want = lax.broadcasted_iota(jnp.int32, (GLOBALS, GLOBALS * TILE), 0) * TILE
-        here = jnp.where(spot == want + col_ref[...] % TILE, 1.0, 0.0).astype(jnp.bfloat16)
+        here = jnp.where(spot == want + column() % TILE, 1.0, 0.0).astype(jnp.bfloat16)
         for pair in range(PAIRS):
             lanes = slice(pair * LANES, (pair + 1) * LANES)
             far_k = join_pair(dil_k[2 * pair], dil_k[2 * pair + 1])
@@ -176,7 +185,7 @@
 
         for group in range(GLOBALS // SLOTS):
 
-            @pl.when(count > group * SLOTS)
+            @pl.when(owns[0] > group * SLOTS)
             def _():
                 ratio = acc[group] / total[group]
                 ratio = jnp.where(head_mask(ratio.shape), ratio, 0.0).astype(jnp.bfloat16)
@@ -190,11 +199,8 @@
     tok, width = queries.shape
     length = keys.shape[0]
     groups = GLOBALS // SLOTS
-    me = lax.axis_index("seq").astype(jnp.int32)
-    count = jnp.sum((global_rows // tok == me).astype(jnp.int32))
-    scal = jnp.concatenate([dilation, me[None], count[None], global_rows])
-    whole = lambda shape: pl.BlockSpec(shape, lambda i, s: (0, 0))
-    chunked = pl.BlockSpec((CHUNK, width), lambda i, s: (i, 0))
+    whole = lambda shape: pl.BlockSpec(shape, lambda i, d, s: (0, 0))
+    chunked = pl.BlockSpec((CHUNK, width), lambda i, d, s: (i, 0))
     raw = pl.BlockSpec(memory_space=pl.ANY)
     far = pltpu.VMEM((H, tok, LANES), jnp.bfloat16)
     near = pltpu.VMEM((tok + 2 * BLK, width), jnp.bfloat16)
@@ -204,10 +210,10 @@
         functools.partial(attention_kernel, length),
         out_shape=jax.ShapeDtypeStruct((tok, width), jnp.bfloat16),
         grid_spec=pltpu.PrefetchScalarGridSpec(
-            num_scalar_prefetch=1,
+            num_scalar_prefetch=2,
             grid=(length // CHUNK,),
             in_specs=[
-                whole((tok, width)), whole((GLOBALS, 1)), whole((1, GLOBALS)),
+                whole((tok, width)), whole((1, GLOBALS)),
                 chunked, chunked, raw, raw,
             ],
             out_specs=whole((tok, width)),
@@ -216,6 +222,7 @@
                 pltpu.VMEM((groups, H * SLOTS, width), jnp.bfloat16),
                 state, state,
                 pltpu.VMEM((groups, H * SLOTS, width), jnp.float32),
+                pltpu.SMEM((1,), jnp.int32),
                 pltpu.SemaphoreType.DMA((2 * (H + 3) + 2,)),
             ],
         ),
@@ -223,7 +230,7 @@
         cost_estimate=pl.CostEstimate(
             flops=20_000_000_000, bytes_accessed=4 * length * width, transcendentals=5_000_000
         ),
-    )(scal, queries, global_rows[:, None], global_rows[None, :], keys, values, keys, values)
+    )(dilation, global_rows, queries, global_rows[None, :], keys, values, keys, values)
 
 
 MESH = pl.DeviceIdType.MESH
@@ -338,9 +345,6 @@
     for at in (0, 1):
         for way in range(2):
             ring_start(at, way, 1)
-    for at in (2, 3):
-        for way in range(2):
-            ring_start(at, way, 1)
     for at in range(4):
         core_start(at, pos, None, None, ins[at])
         copy = pltpu.make_async_copy(ins[at], held(at, pos, None, None), own_sems.at[at])
@@ -360,6 +364,10 @@
         if hop <= half:
             ring_step(0, hop)
             ring_step(1, hop)
+        if hop == 1:
+            for at in (2, 3):
+                for way in range(2):
+                    ring_start(at, way, 1)
         if hop > 1:
             ring_step(2, hop - 1)
             ring_step(3, hop - 1)

time: 153 us -> 148 us (0.967)
  other arithmetic: 3.42 us -> 0 us
    concatenate x1 -> x0, other arithmetic: 1.97 us -> none  [attention(): scal = jnp.concatenate([dilation, me[None], count[None], global_rows])]
where the time goes in v4:
time: 148 us
  Pallas kernels  133 us (90%)
  matrix products  14.5 us (10%)
    pallas_call x1, Pallas kernels, gathered(): pl.pallas_call(functools.partial(gather_kernel, chips), out_shape=[jax.Sh...  113 us
    pallas_call x1, Pallas kernels, attention(): pl.pallas_call(functools.partial(attention_kernel, length), out_shape=jax...  19.8 us
    dot_general x1, matrix products, per_device(): jnp.dot(hidden, down, preferred_element_type=jnp.float32)  12.7 us

profile of v4, /device:TPU:1, one launch (start us, length us, event | category | flops | bytes accessed | tf_op | source)
XLA Modules:
  0.0 148.0 jit_solution(12390644365807357937)
XLA Ops:
  0.6 0.0 copy-start
  0.6 113.0 %shard_map.95 = (bf16[1536,3072]{1,0:T(8,128)(2,1)}, bf16[3072,1536]{1,0:T(8,128)(2,1)}, bf16[4096,768]{1,0:T(8,128)(2,1)}, bf16[4096,768]{1,0:T(8,128)(2,1)}) custom-call(bf16[96,3072]{1,0:T(8,128)(2,1)} %refs_0_.1, bf16[192,1536]{1,0:T(8,128)(2,1)} %refs_1_.1, bf16[256,768]{1,0:T(8,128)(2,1)} %refs_2_.1, bf16[256,768]{1,0:T(8,128)(2,1)} %refs_3_.1), custom_call_target="tpu_custom_call" | custom-call | tf_op jit(solution)/shard_map/pallas_call | solution.py:393
  113.7 19.8 %shard_map.96 = bf16[256,768]{1,0:T(8,128)(2,1)} custom-call(s32[12]{0:T(128)} %dilation.1, s32[64]{0:T(128)} %spots.1, bf16[256,768]{1,0:T(8,128)(2,1)} %q_ref.1, s32[1,64]{1,0:T(1,128)} %bitcast.6, bf16[4096,768]{1,0:T(8,128)(2,1)} %get-tuple-element.6.kc_ref.k_hbm, bf16[4096,768]{1,0:T(8,128)(2,1)} %get-tuple-element.7.vc_ref.v_hbm, ...), custom_call_target="tpu_custom_call" | custom-call | flops 20000000000 | bytes 12582912 | tf_op jit(solution)/shard_map/pallas_call | solution.py:209
  133.5 0.0 copy-done
  133.5 1.8 %convolution_convert_fusion.1 = bf16[256,1536]{1,0:T(8,128)(2,1)S(1)} fusion(bf16[256,768]{1,0:T(8,128)(2,1)} %shard_map.96, bf16[768,1536]{1,0:T(8,128)(2,1)S(1)} %copy-done), kind=kOutput, calls=%fused_computation.10 | convolution fusion | flops 604372992 | bytes 3538944 | tf_op jit(solution)/shard_map/dot_general | solution.py:411
  135.3 0.0 copy-start.1
  135.3 12.7 %convolution_convert_fusion = bf16[256,1536]{1,0:T(8,128)(2,1)} fusion(bf16[3072,1536]{1,0:T(8,128)(2,1)} %get-tuple-element.9, bf16[256,1536]{1,0:T(8,128)(2,1)S(1)} %convolution_convert_fusion.1, bf16[1536,3072]{1,0:T(8,128)(2,1)} %get-tuple-element.8), kind=kOutput, calls=%fused_computation.9 | convolution fusion | flops 4839309312 | bytes 20447232 | tf_op jit(solution)/shard_map/dot_general | solution.py:414
  148.0 0.0 copy-done.1
Async XLA Ops:
  0.6 132.9 %copy-start = (bf16[768,1536]{1,0:T(8,128)(2,1)S(1)}, bf16[768,1536]{1,0:T(8,128)(2,1)}, u32[]{:S(2)}) copy-start(bf16[768,1536]{1,0:T(8,128)(2,1)} %param.13) | copy-start | bytes 7077892
  135.3 12.7 %copy-start.1 = (bf16[256,1536]{1,0:T(8,128)(2,1)}, bf16[256,1536]{1,0:T(8,128)(2,1)S(1)}, u32[]{:S(2)}) copy-start(bf16[256,1536]{1,0:T(8,128)(2,1)S(1)} %convolution_convert_fusion.1) | copy-start | bytes 2359300
